TPU v7x, 128 devices: a whole 4x4x4 slice. The times are simulated.
128 devices in a mesh: chan: 8 (over x, z_hi), row: 4 (over y), col: 4 (over z_lo, core).
Axes of the slice: x: 4, y: 4, z: 4 (z_hi: 2, z_lo: 2; z = z_hi * 2 + z_lo), core: 2. Of those that a mesh axis runs over, the one named last changes fastest.
Arguments:
- voltages: bfloat16 [2, 4, 512, 64, 1031], P(None, None, ('chan', 'row', 'col')), may hold values from -6 to 6
- window: float32 [8, 64], replicated, may hold values from 0.1 to 0.6
- kept_channels: int32 [48], replicated, may hold values from 0 to 63, as said below
Outputs:
- covariance: float32 [48, 2, 2048, 2048], P('chan', None, 'row', 'col')
Inputs may be any that keep to these rules, and one draw needn't show every extreme that they name: `kept_channels`: 48 distinct channel numbers of the 64-point transform, in any order.
All inputs are finite; a program needn't handle non-finite values.
Results may differ from a plain program's by a relative error of at most 0.0019.
Values may be sent and summed in bfloat16 or wider, within the bound.
No kernel may reach another device: no remote copies, remote signals or barrier semaphores. Data moves between devices by JAX's collectives and lax.ppermute only.
A program may use at most 128 MiB of HBM per device.

v0:
```python
import math
import jax
import jax.numpy as jnp
from jax import lax
from jax.sharding import Mesh
from jax.sharding import PartitionSpec as P

COL = ("col_0", "col_1")
CHAN_ROW_COL = ("chan", "row", "col_0", "col_1")
ROW_COL = ("row", "col_0", "col_1")


def in_order(tiles, dim):
    shape = list(tiles.shape[1:])
    shape[dim] *= tiles.shape[0]
    return jnp.moveaxis(tiles, 0, dim).reshape(shape)


def gather_in_order(shard, axes, turns):
    tiles = shard[None]
    for k in turns:
        tiles = lax.all_gather(tiles, axes[k], axis=0, tiled=True)
    current = [lax.axis_size(axes[k]) for k in reversed(turns)]
    tiles = tiles.reshape(*current, *shard.shape)
    turned = sorted(range(len(turns)), key=lambda place: turns[len(turns) - 1 - place])
    return tiles.transpose(*turned, *range(len(turns), tiles.ndim)).reshape(-1, *shard.shape)


def whole_of(shard, axes, turns, dim):
    return in_order(gather_in_order(shard, axes, turns), dim)


def cut_along(shard, dim, peers):
    shape = shard.shape
    tiles = shard.reshape(*shape[:dim], peers, shape[dim] // peers, *shape[dim + 1 :])
    return jnp.moveaxis(tiles, dim, 0)


def exchange_both(shard, axis, axes, splits, concats):
    sizes = [lax.axis_size(a) for a in axes]
    tiles = cut_along(shard, splits[0], sizes[0])
    tiles = jnp.moveaxis(cut_along(tiles, splits[1] + 1, sizes[1]), 0, 1)
    inside = tiles.shape[2:]
    tiles = tiles.reshape(-1, *inside)
    tiles = lax.all_to_all(tiles, axis, split_axis=0, concat_axis=0, tiled=True)
    tiles = in_order(tiles.reshape(*sizes, *inside), concats[0] + 1)
    return in_order(tiles, concats[1])


def phase_table(kept_channels, points):
    positions = jnp.arange(points, dtype=jnp.int32)
    phases = kept_channels[:, None] * positions[None, :] % points
    angles = phases.astype(jnp.float32) * (2.0 * math.pi / points)
    factor = 1.0 / math.sqrt(points)
    cosines = jnp.cos(angles) * factor
    sines = jnp.sin(angles) * factor
    return jnp.stack([jnp.stack([cosines, -sines]), jnp.stack([sines, cosines])])


def filter_bank(samples, window, frames):
    filtered = window[0][:, None] * samples[..., 0:frames]
    for tap_index in range(1, window.shape[0]):
        filtered = (
            filtered + window[tap_index][:, None] * samples[..., tap_index : tap_index + frames]
        )
    return filtered


def products(row_full, col_full):
    real_part = jnp.einsum(
        "bpmif,bpmjf->mij", row_full, col_full, preferred_element_type=jnp.float32
    )
    imag_part = jnp.einsum(
        "bmif,bmjf->mij", row_full[:, 1], col_full[:, 0], preferred_element_type=jnp.float32
    )
    imag_part = imag_part - jnp.einsum(
        "bmif,bmjf->mij", row_full[:, 0], col_full[:, 1], preferred_element_type=jnp.float32
    )
    inverse = 1.0 / (row_full.shape[0] * row_full.shape[4])
    return jnp.stack([real_part, imag_part], axis=1) * inverse


def correlate(pieces):
    row_part, col_part = pieces
    row_full = whole_of(row_part, COL, (0, 1), 0)
    col_full = lax.all_gather(col_part, "row", axis=0, tiled=True)
    return products(row_full, col_full)


def arrange(spectra, shape):
    return (spectra.reshape(shape), jnp.swapaxes(spectra, 1, 2).reshape(shape))


def shards(voltages, window, kept_channels):
    chan_count = lax.axis_size("chan")
    row_count = lax.axis_size("row")
    col_count = lax.axis_size(COL)
    points = window.shape[1]
    frames = voltages.shape[4] - window.shape[0] + 1
    slot_inputs = voltages.shape[2]
    per_chan = kept_channels.shape[0] // chan_count
    block_frames = frames // col_count
    samples = voltages.astype(jnp.float32)
    filtered = filter_bank(samples, window, frames)
    filtered = filtered.reshape(2, row_count, slot_inputs, points, col_count, block_frames)
    table = phase_table(kept_channels, points).reshape(2, 2, chan_count, per_chan, points)
    spectra = jnp.einsum(
        "qrsnbf,qpckn->crbpksf", filtered, table, precision=lax.Precision.HIGHEST
    ).astype(jnp.bfloat16)
    sectioned_shape = (
        chan_count,
        row_count * col_count,
        2,
        per_chan,
        1,
        1,
        slot_inputs,
        block_frames,
    )
    outgoing = arrange(spectra, sectioned_shape)
    arrived = (
        exchange_both(outgoing[0], CHAN_ROW_COL, ("chan", ROW_COL), (0, 1), (4, 5)),
        exchange_both(outgoing[1], CHAN_ROW_COL, ("chan", ROW_COL), (0, 1), (4, 5)),
    )
    arrived = jax.tree.map(lambda piece: piece.reshape(1, 2, per_chan, -1, block_frames), arrived)
    return correlate(arrived)


def solution(mesh):
    finer = Mesh(
        mesh.devices.reshape(mesh.shape["chan"], mesh.shape["row"], 2, 2),
        ("chan", "row", "col_0", "col_1"),
    )
    placed = (P(None, None, CHAN_ROW_COL, None, None), P(), P())
    return jax.shard_map(
        shards, mesh=finer, in_specs=placed, out_specs=P("chan", None, "row", COL), check_vma=False
    )
```

profile of v0, /device:TPU:1, one launch (start us, length us, event | category | flops | bytes accessed | tf_op | source)
XLA Modules:
  0.0 426.3 jit_solution(12734910430916442310)
XLA Ops:
  6.5 0.0 all-gather.4.cloned.1.call-start
  6.5 0.7 mul.173
  7.3 0.1 copy.31
  7.4 1.0 slice_bitcast_fusion.19
  8.3 0.2 fusion.31
  8.5 3.5 convert_element_type.36
  12.0 16.8 %fusion.2 = f32[2,4,4,64,1024]{4,3,2,1,0:T(8,128)} fusion(f32[2,4,4,64,1031]{4,3,2,1,0:T(8,128)S(1)} %convert_element_type.36, f32[64]{0:T(128)S(1)} %get-tuple-element.14, f32[64]{0:T(128)S(1)} %get-tuple-element.15, f32[64]{0:T(128)S(1)} %get-tuple-element.9, f32[64]{0:T(128)S(1)} %get-tuple-element.10, f32[64]{0:T(128)S(1)} %get-tuple-element.11, ...), kind=kLoop, calls=%fused_computation.4 | loop fusion | flops 31457280 | bytes 75499520 | tf_op jit(solution)/shard_map/add | solution.py:64
  28.8 10.6 %reshape.151 = f32[2,4,4,64,4,256]{5,4,3,2,1,0:T(4,128)} reshape(f32[2,4,4,64,1024]{4,3,2,1,0:T(8,128)} %fusion.2) | data formatting | bytes 16777216 | tf_op jit(solution)/shard_map/reshape | solution.py:105
  39.4 9.3 %bitcast_convert_fusion = bf16[2,8,6,4,4,4,256]{6,1,5,4,3,2,0:T(8,128)(2,1)S(1)} fusion(f32[2,4,4,64,4,256,1,1]{5,4,3,2,1,0,7,6:T(4,128)} %bitcast.102, f32[1,1,8,6,64]{4,2,0,3,1:T(8,128)S(1)} %get-tuple-element.7, f32[1,1,8,6,64]{4,2,0,3,1:T(8,128)S(1)} %get-tuple-element.6, f32[1,1,8,6,64]{4,2,0,3,1:T(8,128)S(1)} %get-tuple-element.5), kind=kOutput, calls=%fused_computation.28 | convolution fusion | flops 2417528832 | bytes 11571200 | tf_op jit(solution)/shard_map/qrsnbf,qpckn->crbpksf/dot_general | solution.py:107
  48.7 2.4 copy.33
  51.1 52.5 %all_to_all.10 = bf16[128,1,1,2,6,1,1,4,256]{8,7,4,3,6,5,2,1,0:T(4,128)(2,1)S(1)} all-to-all(bf16[128,1,1,2,6,1,1,4,256]{8,7,4,3,6,5,2,1,0:T(4,128)(2,1)S(1)} %bitcast.101), channel_id=1, replica_groups=mesh['chan'=8,'row'=4,'col_0'=2,'col_1'=2] {'chan','row','col_0','col_1'}, dimensions={0} | all-to-all | bytes 6291456 | tf_op jit(solution)/shard_map/all_to_all | solution.py:45
  103.7 3.3 copy.35
  106.9 2.2 copy.36
  109.1 0.0 all-gather.4.cloned.1.call-update
  109.1 0.0 all-gather.6.cloned.1.call-start
  109.2 79.7 %all-gather.4.cloned.1.call-done = bf16[2,1,2,6,512,256]{5,4,3,2,1,0:T(8,128)(2,1)} async-done(((bf16[1,1,2,6,512,256]{5,4,3,2,1,0:T(8,128)(2,1)}), bf16[2,1,2,6,512,256]{5,4,3,2,1,0:T(8,128)(2,1)}) %all-gather.4.cloned.1.call-update) | async-done | bytes 6291472 | tf_op jit(solution)/shard_map/all_gather | solution.py:22
  188.9 0.0 all-gather.6.cloned.1.call-update
  188.9 0.0 all-gather.8.cloned.1.call-start
  188.9 2.4 copy.38
  191.4 50.3 %all_to_all.11 = bf16[128,1,1,2,6,1,1,4,256]{8,7,4,3,6,5,2,1,0:T(4,128)(2,1)S(1)} all-to-all(bf16[128,1,1,2,6,1,1,4,256]{8,7,4,3,6,5,2,1,0:T(4,128)(2,1)S(1)} %bitcast.99), channel_id=1, replica_groups=mesh['chan'=8,'row'=4,'col_0'=2,'col_1'=2] {'chan','row','col_0','col_1'}, dimensions={0} | all-to-all | bytes 6291456 | tf_op jit(solution)/shard_map/all_to_all | solution.py:45
  241.6 1.7 copy.40
  243.4 3.0 reshape_reshape.7
  246.4 0.0 all-gather.8.cloned.1.call-update
  246.4 0.0 all-gather.6.cloned.1.call-done
  246.5 10.8 %copy.37 = bf16[2,2,1,2,6,512,256]{6,5,3,4,1,0,2:T(8,128)(2,1)} copy(bf16[2,2,1,2,6,512,256]{6,5,4,3,0,1,2:T(8,128)(2,1)} %bitcast.91) | data formatting | bytes 25165824 | tf_op jit(solution)/shard_map/transpose | solution.py:26
  257.3 104.5 %all-gather.8.cloned.1.call-done = bf16[4,2,6,512,256]{4,3,2,1,0:T(8,128)(2,1)} async-done(((bf16[1,2,6,512,256]{4,3,2,1,0:T(8,128)(2,1)}), bf16[4,2,6,512,256]{4,3,2,1,0:T(8,128)(2,1)}) %all-gather.8.cloned.1.call-update) | async-done | bytes 12582928 | tf_op jit(solution)/shard_map/all_gather | solution.py:86
  361.8 10.6 %fusion.11 = f32[6,512,512,1]{2,1,0,3:T(8,128)} fusion(bf16[4,2,6,512,256]{4,3,2,1,0:T(8,128)(2,1)} %all-gather.8.cloned.1.call-done, bf16[4,2,6,512,256]{4,3,1,2,0:T(8,128)(2,1)} %bitcast.92), kind=kOutput, calls=%fused_computation.21 | convolution fusion | flops 3221225472 | bytes 18874368 | tf_op jit(solution)/shard_map/bmif,bmjf->mij/dot_general | solution.py:76
  372.4 15.0 %fusion.16 = f32[6,1,512,512]{3,2,0,1:T(8,128)} fusion(bf16[4,2,6,512,256]{4,3,1,2,0:T(8,128)(2,1)} %bitcast.93, bf16[4,2,6,512,256]{4,3,2,1,0:T(8,128)(2,1)} %all-gather.8.cloned.1.call-done), kind=kOutput, calls=%fused_computation.29 | convolution fusion | flops 6442450944 | bytes 31457280 | tf_op jit(solution)/shard_map/bpmif,bpmjf->mij/dot_general | solution.py:70
  387.4 0.0 copy-start
  387.4 12.6 %fusion.13 = f32[6,1,512,512]{3,2,0,1:T(8,128)} fusion(f32[6,512,512,1]{2,1,0,3:T(8,128)} %fusion.11, bf16[4,2,6,512,256]{4,3,2,1,0:T(8,128)(2,1)} %all-gather.8.cloned.1.call-done, bf16[4,2,6,512,256]{4,3,1,2,0:T(8,128)(2,1)} %bitcast.94), kind=kOutput, calls=%fused_computation.27 | convolution fusion | flops 3222798336 | bytes 25165824 | tf_op jit(solution)/shard_map/bmif,bmjf->mij/dot_general | solution.py:73
  400.0 0.0 copy-done
  400.0 8.9 %maximum_multiply_fusion = f32[6,2,512,512]{3,2,0,1:T(8,128)} fusion(f32[6,1,512,512]{3,2,0,1:T(8,128)} %fusion.13, f32[6,1,512,512]{3,2,0,1:T(8,128)S(1)} %copy-done), kind=kLoop, calls=%fused_computation | loop fusion | flops 6291456 | bytes 25165824 | tf_op jit(solution)/shard_map/mul | solution.py:80
  408.9 10.9 %copy.44 = f32[6,2,512,512]{3,2,1,0:T(8,128)} copy(f32[6,2,512,512]{3,2,0,1:T(8,128)} %maximum_multiply_fusion) | data formatting | bytes 25165824 | tf_op jit(solution)/shard_map/mul | solution.py:80
Async XLA Ops:
  6.5 182.3 %all-gather.4.cloned.1.call-start = ((), (), s32[]{:S(2)}) async-start(), calls=%async_computation.2 | async-start | bytes 9437184 | tf_op jit(solution)/shard_map/all_gather | solution.py:22
  109.1 137.3 %all-gather.6.cloned.1.call-start = ((), (), s32[]{:S(2)}) async-start(), calls=%async_computation.3 | async-start | bytes 18874368 | tf_op jit(solution)/shard_map/all_gather | solution.py:22
  188.9 172.9 %all-gather.8.cloned.1.call-start = ((), (), s32[]{:S(2)}) async-start(), calls=%async_computation.4 | async-start | bytes 15728640 | tf_op jit(solution)/shard_map/all_gather | solution.py:86
  387.4 12.6 %copy-start = (f32[6,1,512,512]{3,2,0,1:T(8,128)S(1)}, f32[6,1,512,512]{3,2,0,1:T(8,128)}, u32[]{:S(2)}) copy-start(f32[6,1,512,512]{3,2,0,1:T(8,128)} %fusion.16) | copy-start | bytes 18874372
Sparse Core Ops, SparseCore 0:
  109.2 79.5 all-gather.3
  190.5 28.9 all-gather.5
  246.6 115.1 all-gather.7
where the time goes:
time: 427 us; the launch traced here: 426 us
  waiting for transfers between devices  184 us (43%)
  blocking collectives  103 us (24%)
  local copies, waits for them, and re-layouts  49.1 us (11%)
  matrix products  47.5 us (11%)
  other arithmetic  29.4 us (7%)
  between operations  13.2 us (3%)
    all_gather x1, waiting for transfers between devices, correlate(): col_full = lax.all_gather(col_part, 'row', axis=0, tiled=True)  105 us
    all_to_all x2, blocking collectives, exchange_both(): tiles = lax.all_to_all(tiles, axis, split_axis=0, concat_axis=0, tiled=True)  103 us
    all_gather x2, waiting for transfers between devices, gather_in_order(): tiles = lax.all_gather(tiles, axes[k], axis=0, tiled=True)  79.7 us
    add x1, other arithmetic, filter_bank(): filtered + window[tap_index][:, None] * samples[..., tap_index:tap_index...  16.8 us
    dot_general x1, matrix products, products(): jnp.einsum('bpmif,bpmjf->mij', row_full, col_full, preferred_element_type...  15 us
    dot_general x1, matrix products, products(): jnp.einsum('bmif,bmjf->mij', row_full[:, 1], col_full[:, 0], preferred_el...  12.6 us
    mul x1, local copies, waits for them, and re-layouts, products(): return jnp.stack([real_part, imag_part], axis=1) * inverse  10.9 us
    transpose x1, local copies, waits for them, and re-layouts, gather_in_order(): tiles.transpose(*turned, *range(len(turns), tiles.ndim))  10.8 us
  transfers between devices with their start and end apart: 3, of which 2 were waited for; matrix products, arithmetic and copies ran while one was open for 4% of the time, Pallas kernels for 0%

commit v1 on v0

--- a/solution.py
+++ b/solution.py
@@ -83,7 +83,8 @@
 def correlate(pieces):
     row_part, col_part = pieces
     row_full = whole_of(row_part, COL, (0, 1), 0)
-    col_full = lax.all_gather(col_part, "row", axis=0, tiled=True)
+    local_next = jnp.concatenate([col_part for _ in range(lax.axis_size("row"))], axis=0)
+    col_full = lax.all_to_all(local_next, "row", 0, 0, tiled=True)
     return products(row_full, col_full)
 
 

time: 427 us -> 462 us (1.082)
  waiting for transfers between devices: 184 us -> 207 us
  starting transfers between devices: 0.08 us -> 6.56 us
    all_to_all x0 -> x1, waiting for transfers between devices: none -> 127 us  [correlate(): col_full = lax.all_to_all(local_next, 'row', 0, 0, tiled=True)]
    all_gather x1 -> x0, waiting for transfers between devices: 105 us -> none  [correlate(): col_full = lax.all_gather(col_part, 'row', axis=0, tiled=True)]
    all_to_all x0 -> x1, starting transfers between devices: none -> 6.52 us  [correlate(): col_full = lax.all_to_all(local_next, 'row', 0, 0, tiled=True)]
    concatenate x0 -> x1, local copies, waits for them, and re-layouts: none -> 6.27 us  [correlate(): jnp.concatenate([col_part for _ in range(lax.axis_size('row'))], axis=0)]
  transfers between devices with their start and end apart: 3 -> 3, of which waited for: 2 -> 2; matrix products, arithmetic and copies ran while one was open for 4% -> 5% of each run, Pallas kernels for 0% -> 0%
where the time goes in v1:
time: 462 us; the launch traced here: 460 us
  waiting for transfers between devices  207 us (45%)
  blocking collectives  103 us (22%)
  local copies, waits for them, and re-layouts  53.4 us (12%)
  matrix products  47.9 us (10%)
  other arithmetic  29.4 us (6%)
  between operations  13.5 us (3%)
  starting transfers between devices  6.56 us (1%)
    all_to_all x1, waiting for transfers between devices, correlate(): col_full = lax.all_to_all(local_next, 'row', 0, 0, tiled=True)  127 us
    all_to_all x2, blocking collectives, exchange_both(): tiles = lax.all_to_all(tiles, axis, split_axis=0, concat_axis=0, tiled=True)  103 us
    all_gather x2, waiting for transfers between devices, gather_in_order(): tiles = lax.all_gather(tiles, axes[k], axis=0, tiled=True)  79.7 us
    add x1, other arithmetic, filter_bank(): filtered + window[tap_index][:, None] * samples[..., tap_index:tap_index...  16.8 us
    dot_general x1, matrix products, products(): jnp.einsum('bpmif,bpmjf->mij', row_full, col_full, preferred_element_type...  15 us
    dot_general x1, matrix products, products(): jnp.einsum('bmif,bmjf->mij', row_full[:, 1], col_full[:, 0], preferred_el...  12.7 us
    dot_general x1, matrix products, products(): jnp.einsum('bmif,bmjf->mij', row_full[:, 0], col_full[:, 1], preferred_el...  10.9 us
    mul x1, local copies, waits for them, and re-layouts, products(): return jnp.stack([real_part, imag_part], axis=1) * inverse  10.9 us
  transfers between devices with their start and end apart: 3, of which 2 were waited for; matrix products, arithmetic and copies ran while one was open for 5% of the time, Pallas kernels for 0%

profile of v1, /device:TPU:1, one launch (start us, length us, event | category | flops | bytes accessed | tf_op | source)
XLA Modules:
  0.0 460.5 jit_solution(16868476523145801715)
XLA Ops:
  6.5 0.0 all-gather.3.cloned.1.call-start
  6.5 1.0 slice_bitcast_fusion.19
  7.5 3.5 convert_element_type.36
  11.0 16.8 %fusion = f32[2,4,4,64,1024]{4,3,2,1,0:T(8,128)} fusion(f32[2,4,4,64,1031]{4,3,2,1,0:T(8,128)S(1)} %convert_element_type.36, f32[64]{0:T(128)S(1)} %get-tuple-element.14, f32[64]{0:T(128)S(1)} %get-tuple-element.15, f32[64]{0:T(128)S(1)} %get-tuple-element.9, f32[64]{0:T(128)S(1)} %get-tuple-element.10, f32[64]{0:T(128)S(1)} %get-tuple-element.11, ...), kind=kLoop, calls=%fused_computation.2 | loop fusion | flops 31457280 | bytes 75499520 | tf_op jit(solution)/shard_map/add | solution.py:64
  27.8 0.0 copy-start
  27.8 10.6 %reshape.153 = f32[2,4,4,64,4,256]{5,4,3,2,1,0:T(4,128)} reshape(f32[2,4,4,64,1024]{4,3,2,1,0:T(8,128)} %fusion) | data formatting | bytes 16777216 | tf_op jit(solution)/shard_map/reshape | solution.py:106
  38.4 0.0 copy-done
  38.4 0.1 mul.173
  38.5 0.1 copy.30
  38.6 0.2 fusion.26
  38.8 9.3 %bitcast_convert_fusion = bf16[2,8,6,4,4,4,256]{6,1,5,4,3,2,0:T(8,128)(2,1)S(1)} fusion(f32[2,4,4,64,4,256,1,1]{5,4,3,2,1,0,7,6:T(4,128)} %bitcast.103, f32[1,1,8,6,64]{4,2,0,3,1:T(8,128)S(1)} %get-tuple-element.7, f32[1,1,8,6,64]{4,2,0,3,1:T(8,128)S(1)} %get-tuple-element.6, f32[1,1,8,6,64]{4,2,0,3,1:T(8,128)S(1)} %get-tuple-element.5), kind=kOutput, calls=%fused_computation.26 | convolution fusion | flops 2417528832 | bytes 11571200 | tf_op jit(solution)/shard_map/qrsnbf,qpckn->crbpksf/dot_general | solution.py:108
  48.1 2.4 copy.32
  50.5 52.5 %all_to_all.15 = bf16[128,1,1,2,6,1,1,4,256]{8,7,4,3,6,5,2,1,0:T(4,128)(2,1)S(1)} all-to-all(bf16[128,1,1,2,6,1,1,4,256]{8,7,4,3,6,5,2,1,0:T(4,128)(2,1)S(1)} %bitcast.102), channel_id=1, replica_groups=mesh['chan'=8,'row'=4,'col_0'=2,'col_1'=2] {'chan','row','col_0','col_1'}, dimensions={0} | all-to-all | bytes 6291456 | tf_op jit(solution)/shard_map/all_to_all | solution.py:45
  103.0 3.3 copy.34
  106.3 2.2 copy.35
  108.5 0.0 all-gather.3.cloned.1.call-update
  108.5 0.0 all-gather.5.cloned.1.call-start
  108.5 79.7 %all-gather.3.cloned.1.call-done = bf16[2,1,2,6,512,256]{5,4,3,2,1,0:T(8,128)(2,1)} async-done(((bf16[1,1,2,6,512,256]{5,4,3,2,1,0:T(8,128)(2,1)}), bf16[2,1,2,6,512,256]{5,4,3,2,1,0:T(8,128)(2,1)}) %all-gather.3.cloned.1.call-update) | async-done | bytes 6291472 | tf_op jit(solution)/shard_map/all_gather | solution.py:22
  188.2 0.0 all-gather.5.cloned.1.call-update
  188.3 2.4 copy.37
  190.7 50.3 %all_to_all.16 = bf16[128,1,1,2,6,1,1,4,256]{8,7,4,3,6,5,2,1,0:T(4,128)(2,1)S(1)} all-to-all(bf16[128,1,1,2,6,1,1,4,256]{8,7,4,3,6,5,2,1,0:T(4,128)(2,1)S(1)} %bitcast.99), channel_id=1, replica_groups=mesh['chan'=8,'row'=4,'col_0'=2,'col_1'=2] {'chan','row','col_0','col_1'}, dimensions={0} | all-to-all | bytes 6291456 | tf_op jit(solution)/shard_map/all_to_all | solution.py:45
  241.0 3.3 copy.39
  244.2 0.5 copy.40
  244.8 6.3 %concatenate.6 = bf16[4,2,6,512,256]{4,3,1,2,0:T(8,128)(2,1)} broadcast(bf16[2,6,512,256]{3,2,0,1:T(8,128)(2,1)S(1)} %copy.40), dimensions={1,2,3,4} | broadcast | bytes 15728640 | tf_op jit(solution)/shard_map/concatenate | solution.py:86
  251.0 6.5 %all-to-all-start.2 = ((bf16[4,2,6,512,256]{4,3,1,2,0:T(8,128)(2,1)}), bf16[4,2,6,512,256]{4,3,1,2,0:T(8,128)(2,1)}, u32[]{:S(2)}, u32[]{:S(2)}) async-start(bf16[4,2,6,512,256]{4,3,1,2,0:T(8,128)(2,1)} %concatenate.6), calls=%async_computation.2 | async-start | bytes 25165824 | tf_op jit(solution)/shard_map/all_to_all | solution.py:87
  257.5 0.0 all-gather.5.cloned.1.call-done
  257.6 10.5 %copy.36 = bf16[2,2,1,2,6,512,256]{6,5,3,4,1,0,2:T(8,128)(2,1)} copy(bf16[2,2,1,2,6,512,256]{6,5,4,3,0,1,2:T(8,128)(2,1)} %bitcast.91) | data formatting | bytes 25165824 | tf_op jit(solution)/shard_map/transpose | solution.py:26
  268.1 127.2 %all-to-all-done.2 = bf16[4,2,6,512,256]{4,3,1,2,0:T(8,128)(2,1)} async-done(((bf16[4,2,6,512,256]{4,3,1,2,0:T(8,128)(2,1)}), bf16[4,2,6,512,256]{4,3,1,2,0:T(8,128)(2,1)}, u32[]{:S(2)}, u32[]{:S(2)}) %all-to-all-start.2) | async-done | bytes 12582944 | tf_op jit(solution)/shard_map/all_to_all | solution.py:87
  395.2 15.0 %convolution_bitcast_fusion = f32[6,1,512,512]{3,2,0,1:T(8,128)} fusion(bf16[4,2,6,512,256]{4,3,1,2,0:T(8,128)(2,1)} %bitcast.92, bf16[4,2,6,512,256]{4,3,1,2,0:T(8,128)(2,1)} %all-to-all-done.2), kind=kOutput, calls=%fused_computation.27 | convolution fusion | flops 6442450944 | bytes 31457280 | tf_op jit(solution)/shard_map/bpmif,bpmjf->mij/dot_general | solution.py:70
  410.2 0.0 slice-start
  410.2 10.9 %fusion.9 = f32[6,512,512,1]{2,1,0,3:T(8,128)} fusion(bf16[4,2,6,512,256]{4,3,1,2,0:T(8,128)(2,1)} %all-to-all-done.2, bf16[4,2,6,512,256]{4,3,1,2,0:T(8,128)(2,1)} %bitcast.93), kind=kOutput, calls=%fused_computation.19 | convolution fusion | flops 3221225472 | bytes 18874368 | tf_op jit(solution)/shard_map/bmif,bmjf->mij/dot_general | solution.py:76
  421.1 0.0 slice-start.1
  421.1 12.7 %fusion.11 = f32[6,1,512,512]{3,2,0,1:T(8,128)} fusion(f32[6,512,512,1]{2,1,0,3:T(8,128)} %fusion.9, bf16[4,2,6,512,256]{4,3,1,2,0:T(8,128)(2,1)} %all-to-all-done.2, bf16[4,2,6,512,256]{4,3,1,2,0:T(8,128)(2,1)} %bitcast.94), kind=kOutput, calls=%fused_computation.25 | convolution fusion | flops 3222798336 | bytes 25165824 | tf_op jit(solution)/shard_map/bmif,bmjf->mij/dot_general | solution.py:73
  433.8 0.0 slice-done
  433.8 0.0 slice-done.1
  433.8 8.9 %maximum_multiply_fusion = f32[6,2,512,512]{3,2,0,1:T(8,128)} fusion(f32[6,1,512,512]{3,2,0,1:T(8,128)} %fusion.11, f32[6,1,512,512]{3,2,0,1:T(8,128)S(1)} %bitcast.105), kind=kLoop, calls=%fused_computation | loop fusion | flops 6291456 | bytes 25165824 | tf_op jit(solution)/shard_map/mul | solution.py:80
  442.7 10.9 %copy.43 = f32[6,2,512,512]{3,2,1,0:T(8,128)} copy(f32[6,2,512,512]{3,2,0,1:T(8,128)} %maximum_multiply_fusion) | data formatting | bytes 25165824 | tf_op jit(solution)/shard_map/mul | solution.py:80
  (1 shorter events, 0.0 us)
Async XLA Ops:
  6.5 181.7 %all-gather.3.cloned.1.call-start = ((), (), s32[]{:S(2)}) async-start(), calls=%async_computation.3 | async-start | bytes 9437184 | tf_op jit(solution)/shard_map/all_gather | solution.py:22
  27.8 10.6 %copy-start = (s32[48]{0:T(128)S(1)}, s32[48]{0:T(128)}, u32[]{:S(2)}) copy-start(s32[48]{0:T(128)} %param.5) | copy-start | bytes 580
  108.5 149.1 %all-gather.5.cloned.1.call-start = ((), (), s32[]{:S(2)}) async-start(), calls=%async_computation.4 | async-start | bytes 18874368 | tf_op jit(solution)/shard_map/all_gather | solution.py:22
  251.0 144.2 %all-to-all-start.2 = ((bf16[4,2,6,512,256]{4,3,1,2,0:T(8,128)(2,1)}), bf16[4,2,6,512,256]{4,3,1,2,0:T(8,128)(2,1)}, u32[]{:S(2)}, u32[]{:S(2)}) async-start(bf16[4,2,6,512,256]{4,3,1,2,0:T(8,128)(2,1)} %concatenate.6), calls=%async_computation.2 | async-start | bytes 25165824 | tf_op jit(solution)/shard_map/all_to_all | solution.py:87
  410.2 23.6 %slice-start = ((s8[6291456]{0:T(1024)(128)(4,1)}), s8[4194304]{0:T(1024)(128)(4,1)S(1)}, s32[]{:S(2)}) async-start(s8[6291456]{0:T(1024)(128)(4,1)} %bitcast.104), calls=%async_computation.5 | async-start | bytes 8388608
  421.1 12.7 %slice-start.1 = ((s8[6291456]{0:T(1024)(128)(4,1)}), s8[2097152]{0:T(1024)(128)(4,1)S(1)}, s32[]{:S(2)}) async-start(s8[6291456]{0:T(1024)(128)(4,1)} %bitcast.104), calls=%async_computation.6 | async-start | bytes 4194304
Sparse Core Ops, SparseCore 0:
  108.6 79.5 all-gather.2
  189.9 28.9 all-gather.4
